TPU v7x, 512 devices: a whole 4x4x16 slice. The times are simulated.
512 devices in a mesh: doc: 8 (over y, core), label: 64 (over z, x).
Axes of the slice: x: 4, y: 4, z: 16, core: 2. Of those that a mesh axis runs over, the one named last changes fastest.
Arguments:
- features: float32 [4096, 1024], P('doc'), may hold values from -6 to 6
- doc_labels: int32 [4096, 16], P('doc'), may hold values from 0 to 16383, all different within a row
- tree_perm: int32 [16384], replicated, may hold values from 0 to 16383, as said below
- cluster_sizes: int32 [512], replicated, may hold values from 1 to 4096, 16384 in all
Outputs:
- scores: float32 [4096, 16384], P('doc', 'label')
Inputs may be any that keep to these rules, and one draw needn't show every extreme that they name: `doc_labels`: each document names 16 different labels, and every label is named by some document. `tree_perm`: a permutation; every aligned block of 256 tree positions holds exactly 4 labels of every aligned block of 256 natural indices. `cluster_sizes`: the sizes sum to 16384; the largest is exactly 4096.
All inputs are finite; a program needn't handle non-finite values.
Results may differ from a plain program's by a relative error of at most 0.0001.
Values sent between devices are 32-bit elements; how exact they have to be, the bound alone decides.
No kernel may reach another device: no remote copies, remote signals or barrier semaphores. Data moves between devices by JAX's collectives and lax.ppermute only.
A program may use at most 64 MiB of HBM per device.

v0:
```python
import jax
import jax.numpy as jnp
from jax import lax
from jax.sharding import PartitionSpec as P

L_DEV = 256
EPS = 1e-06


def unit_rows(matrix):
    return matrix * lax.rsqrt(jnp.sum(matrix * matrix, axis=1, keepdims=True) + EPS)


def cluster_of(positions, starts):
    return jnp.sum((starts[None, 1:] <= positions[:, None]).astype(jnp.int32), axis=1)


def shards(features, doc_labels, tree_perm, cluster_sizes):
    width = lax.axis_size("label")
    here = lax.axis_index("label")
    base = here * L_DEV
    slots = jnp.arange(L_DEV, dtype=jnp.int32)
    own_perm = lax.dynamic_slice_in_dim(tree_perm, base, L_DEV)
    incidence = jnp.sum(
        (doc_labels[:, :, None] == own_perm[None, None, :]).astype(jnp.float32), axis=1
    )
    partial_value = lax.dot_general(
        incidence,
        features,
        (((0,), (0,)), ((), ())),
        precision=lax.Precision.HIGHEST,
        preferred_element_type=jnp.float32,
    )
    summed = lax.psum(partial_value, "doc")
    label_rows = unit_rows(summed)
    starts = jnp.cumsum(cluster_sizes) - cluster_sizes
    cluster_ids = cluster_of(base + slots, starts)
    shard = jnp.arange(width, dtype=jnp.int32)
    first_id = cluster_of(shard * L_DEV, starts)
    last_id = cluster_of(shard * L_DEV + (L_DEV - 1), starts)
    same_cluster = (cluster_ids[:, None] == cluster_ids[None, :]).astype(jnp.float32)
    local_sum = jnp.dot(
        same_cluster,
        label_rows,
        precision=lax.Precision.HIGHEST,
        preferred_element_type=jnp.float32,
    )
    ends = jnp.stack([local_sum[0], local_sum[-1]])
    gathered = lax.all_gather(ends, "label").reshape(2 * width, -1)
    other = (shard != here)[None, :]
    take_first = (first_id[None, :] == cluster_ids[:, None]) & other
    take_last = (last_id[None, :] == cluster_ids[:, None]) & (first_id != last_id)[None, :] & other
    weights = jnp.stack([take_first, take_last], axis=2).reshape(L_DEV, 2 * width)
    cluster_sum = local_sum + jnp.dot(
        weights.astype(jnp.float32),
        gathered,
        precision=lax.Precision.HIGHEST,
        preferred_element_type=jnp.float32,
    )
    centroid = unit_rows(cluster_sum)
    combined = label_rows + centroid
    doc_unit = unit_rows(features)
    return lax.dot_general(
        doc_unit,
        combined,
        (((1,), (1,)), ((), ())),
        precision=lax.Precision.HIGHEST,
        preferred_element_type=jnp.float32,
    )


def solution(mesh):
    in_specs = (P("doc", None), P("doc", None), P(), P())
    out_specs = P("doc", "label")
    return jax.shard_map(shards, mesh=mesh, in_specs=in_specs, out_specs=out_specs, check_vma=False)
```

profile of v0, /device:TPU:2, one launch (start us, length us, event | category | flops | bytes accessed | tf_op | source)
XLA Modules:
  0.0 221.0 jit_solution(827182188428001773)
XLA Ops:
  6.5 0.0 all-reduce.2.cloned.1.call-start
  6.5 0.9 copy.11
  7.4 0.8 dynamic_slice.3
  8.2 10.9 %convert_reduce_fusion = f32[512,256]{1,0:T(8,128)S(1)} fusion(s32[256]{0:T(256)S(1)} %dynamic_slice.3, s32[512,16]{1,0:T(8,128)S(1)} %copy.11), kind=kLoop, calls=%fused_computation | loop fusion | flops 6160384 | bytes 558080 | tf_op jit(solution)/shard_map/reduce_sum | solution.py:24
  19.1 0.0 copy-start
  19.1 4.6 %fusion.21 = f32[256,1024]{1,0:T(8,128)} fusion(f32[512,256]{1,0:T(8,128)S(1)} %convert_reduce_fusion, f32[512,1024]{1,0:T(8,128)} %param.4), kind=kOutput, calls=%fused_computation.41 | convolution fusion | flops 1610612736 | bytes 3670016 | tf_op jit(solution)/shard_map/dot_general | solution.py:27
  23.7 0.0 copy-start.2
  23.7 0.0 all-reduce.2.cloned.1.call-update
  23.8 0.0 copy-done
  23.8 0.2 multiply_reduce_fusion
  24.0 0.4 copy-done.2
  24.4 0.3 reduce-window.9
  24.7 0.1 slice.18
  24.8 0.1 slice_reduce_fusion
  24.9 0.1 bitcast_subtract_fusion
  25.0 0.1 slice.20
  25.1 0.2 convert_reduce_fusion.1
  25.3 0.2 convert_reduce_fusion.3
  25.5 0.1 compare_and_fusion
  25.6 80.6 %all-reduce.2.cloned.1.call-done = f32[256,1024]{1,0:T(8,128)} async-done(((f32[256,1024]{1,0:T(8,128)}), f32[256,1024]{1,0:T(8,128)}) %all-reduce.2.cloned.1.call-update) | async-done | bytes 1048592 | tf_op jit(solution)/shard_map/psum | solution.py:34
  106.3 1.4 multiply_reduce_fusion.2
  107.7 2.1 fusion.7
  109.7 0.0 copy-start.1
  109.8 100.7 %all-gather.1 = f32[64,2,1024]{2,1,0:T(2,128)S(1)} all-gather(f32[1,2,1024]{2,1,0:T(2,128)S(1)} %maximum_bitcast_fusion), channel_id=2, replica_groups=mesh['doc'=8,'label'=64] {'label'}, dimensions={0}, use_global_device_ids=true | all-gather | bytes 532480 | tf_op jit(solution)/shard_map/all_gather | solution.py:49
  210.5 0.8 multiply_reduce_fusion.1
  211.4 0.0 copy-done.1
  211.4 2.8 %fusion = f32[512,256]{1,0:T(8,128)} fusion(f32[512,1024]{1,0:T(8,128)S(1)} %copy-done, f32[256,1024]{1,0:T(8,128)S(1)} %get-tuple-element.12, f32[512]{0:T(512)S(1)} %add_rsqrt_fusion, f32[256,1024]{1,0:T(8,128)S(1)} %copy-done.1, f32[256]{0:T(256)S(1)} %add_rsqrt_fusion.1, f32[256]{0:T(256)S(1)} %add_rsqrt_fusion.2), kind=kOutput, calls=%fused_computation.1 | convolution fusion | flops 1611923456 | bytes 4722688 | tf_op jit(solution)/shard_map/dot_general | solution.py:63
  (10 shorter events, 0.1 us)
Async XLA Ops:
  6.5 99.7 %all-reduce.2.cloned.1.call-start = ((), (), s32[]{:S(2)}) async-start(), calls=%async_computation | async-start | bytes 2097152 | tf_op jit(solution)/shard_map/psum | solution.py:34
  19.1 4.7 %copy-start = (f32[512,1024]{1,0:T(8,128)S(1)}, f32[512,1024]{1,0:T(8,128)}, u32[]{:S(2)}) copy-start(f32[512,1024]{1,0:T(8,128)} %param.4) | copy-start | bytes 6291460
  23.7 0.7 copy-start.2
  109.7 101.6 %copy-start.1 = (f32[256,1024]{1,0:T(8,128)S(1)}, f32[256,1024]{1,0:T(8,128)}, u32[]{:S(2)}) copy-start(f32[256,1024]{1,0:T(8,128)} %all-reduce.2.cloned.1.call-done) | copy-start | bytes 3145732
Sparse Core Ops, SparseCore 0:
  23.9 82.3 all-reduce.1
where the time goes:
time: 221 us
  blocking collectives  101 us (46%)
  waiting for transfers between devices  80.6 us (36%)
  between operations  13.5 us (6%)
  other arithmetic  13.4 us (6%)
  matrix products  10.4 us (5%)
  local copies, waits for them, and re-layouts  2.34 us (1%)
    all_gather x1, blocking collectives, shards(): gathered = lax.all_gather(ends, 'label').reshape(2 * width, -1)  101 us
    psum x1, waiting for transfers between devices, shards(): summed = lax.psum(partial_value, 'doc')  80.6 us
    reduce_sum x1, other arithmetic, shards(): jnp.sum((doc_labels[:, :, None] == own_perm[None, None, :]).astype(jnp.fl...  10.9 us
    dot_general x1, matrix products, shards(): lax.dot_general(incidence, features, (((0,), (0,)), ((), ())), precision=...  4.64 us
  transfers between devices with their start and end apart: 1, of which 1 were waited for; matrix products, arithmetic and copies ran while one was open for 1% of the time, Pallas kernels for 0%

commit v1 on v0

--- a/solution.py
+++ b/solution.py
@@ -5,6 +5,11 @@
 
 L_DEV = 256
 EPS = 1e-06
+
+
+def summed_here(shard, mesh_axis):
+    parts = lax.all_gather(shard, mesh_axis)
+    return jnp.sum(parts, axis=0)
 
 
 def unit_rows(matrix):
@@ -31,7 +36,7 @@
         precision=lax.Precision.HIGHEST,
         preferred_element_type=jnp.float32,
     )
-    summed = lax.psum(partial_value, "doc")
+    summed = summed_here(partial_value, "doc")
     label_rows = unit_rows(summed)
     starts = jnp.cumsum(cluster_sizes) - cluster_sizes
     cluster_ids = cluster_of(base + slots, starts)

time: 221 us -> 203 us (0.919)
  the two profiles are of different devices: /device:TPU:2 before, /device:TPU:4 now
where the time goes in v1:
time: 203 us; the launch traced here: 202 us
  blocking collectives  101 us (50%)
  waiting for transfers between devices  60.5 us (30%)
  other arithmetic  16.6 us (8%)
  between operations  13.5 us (7%)
  matrix products  9.18 us (5%)
    all_gather x1, blocking collectives, shards(): gathered = lax.all_gather(ends, 'label').reshape(2 * width, -1)  101 us
    all_gather x1, waiting for transfers between devices, summed_here(): parts = lax.all_gather(shard, mesh_axis)  60.5 us
    reduce_sum x1, other arithmetic, shards(): jnp.sum((doc_labels[:, :, None] == own_perm[None, None, :]).astype(jnp.fl...  10.9 us
    dot_general x1, matrix products, shards(): lax.dot_general(incidence, features, (((0,), (0,)), ((), ())), precision=...  4.68 us
    reduce_sum x1, other arithmetic, summed_here(): return jnp.sum(parts, axis=0)  4.38 us
  transfers between devices with their start and end apart: 1, of which 1 were waited for; matrix products, arithmetic and copies ran while one was open for 1% of the time, Pallas kernels for 0%

profile of v1, /device:TPU:4, one launch (start us, length us, event | category | flops | bytes accessed | tf_op | source)
XLA Modules:
  0.0 202.4 jit_solution(16440744930831291918)
XLA Ops:
  6.5 0.0 all-gather.5.cloned.1.call-start
  6.5 0.9 copy.11
  7.4 0.8 dynamic_slice.3
  8.2 10.9 %convert_reduce_fusion = f32[512,256]{1,0:T(8,128)S(1)} fusion(s32[256]{0:T(256)S(1)} %dynamic_slice.3, s32[512,16]{1,0:T(8,128)S(1)} %copy.11), kind=kLoop, calls=%fused_computation | loop fusion | flops 6160384 | bytes 558080 | tf_op jit(solution)/shard_map/reduce_sum | solution.py:29
  19.1 0.0 copy-start.1
  19.1 0.0 copy-start
  19.1 4.7 %fusion.21 = f32[256,1024]{1,0:T(8,128)} fusion(f32[512,256]{1,0:T(8,128)S(1)} %convert_reduce_fusion, f32[512,1024]{1,0:T(8,128)} %param.4), kind=kOutput, calls=%fused_computation.41 | convolution fusion | flops 1610612736 | bytes 3670016 | tf_op jit(solution)/shard_map/dot_general | solution.py:32
  23.8 0.0 all-gather.5.cloned.1.call-update
  23.8 0.0 copy-done.1
  23.8 0.3 reduce-window.9
  24.1 0.1 slice.18
  24.2 0.1 slice_reduce_fusion
  24.3 0.1 bitcast_subtract_fusion
  24.4 0.1 slice.20
  24.5 0.2 convert_reduce_fusion.3
  24.7 0.2 convert_reduce_fusion.1
  24.9 0.0 copy-done
  24.9 0.2 multiply_reduce_fusion
  25.2 0.1 compare_and_fusion
  25.3 60.5 %all-gather.5.cloned.1.call-done = f32[2048,1024]{1,0:T(8,128)} async-done(((f32[256,1024]{1,0:T(8,128)}), f32[2048,1024]{1,0:T(8,128)}) %all-gather.5.cloned.1.call-update) | async-done | bytes 8388624 | tf_op jit(solution)/shard_map/all_gather | solution.py:11
  85.8 4.4 %reduce_sum.74 = f32[256,1024]{1,0:T(8,128)S(1)} reduce(f32[8,256,1024]{2,1,0:T(8,128)} %bitcast.12, f32[]{:T(128)} %constant.7.clone.1), dimensions={0}, to_apply=%region_2.0 | reduce | flops 1835008 | bytes 9437188 | tf_op jit(solution)/shard_map/reduce_sum | solution.py:12
  90.2 0.1 multiply_reduce_fusion.2
  90.3 0.8 fusion.7
  91.2 100.6 %all-gather.2 = f32[64,2,1024]{2,1,0:T(2,128)S(1)} all-gather(f32[1,2,1024]{2,1,0:T(2,128)S(1)} %maximum_bitcast_fusion), channel_id=3, replica_groups=mesh['doc'=8,'label'=64] {'label'}, dimensions={0}, use_global_device_ids=true | all-gather | bytes 532480 | tf_op jit(solution)/shard_map/all_gather | solution.py:54
  191.8 0.8 multiply_reduce_fusion.1
  192.7 2.8 %fusion = f32[512,256]{1,0:T(8,128)} fusion(f32[512,1024]{1,0:T(8,128)S(1)} %copy-done, f32[256,1024]{1,0:T(8,128)S(1)} %get-tuple-element.12, f32[512]{0:T(512)S(1)} %add_rsqrt_fusion, f32[256,1024]{1,0:T(8,128)S(1)} %reduce_sum.74, f32[256]{0:T(256)S(1)} %add_rsqrt_fusion.1, f32[256]{0:T(256)S(1)} %add_rsqrt_fusion.2), kind=kOutput, calls=%fused_computation.1 | convolution fusion | flops 1611923456 | bytes 4722688 | tf_op jit(solution)/shard_map/dot_general | solution.py:68
  (10 shorter events, 0.1 us)
Async XLA Ops:
  6.5 79.3 %all-gather.5.cloned.1.call-start = ((), (), s32[]{:S(2)}) async-start(), calls=%async_computation | async-start | bytes 9437184 | tf_op jit(solution)/shard_map/all_gather | solution.py:11
  19.1 4.7 %copy-start.1 = (s32[512]{0:T(512)S(1)}, s32[512]{0:T(512)}, u32[]{:S(2)}) copy-start(s32[512]{0:T(512)} %param.7) | copy-start | bytes 6148
  19.1 5.9 %copy-start = (f32[512,1024]{1,0:T(8,128)S(1)}, f32[512,1024]{1,0:T(8,128)}, u32[]{:S(2)}) copy-start(f32[512,1024]{1,0:T(8,128)} %param.4) | copy-start | bytes 6291460
Sparse Core Ops, SparseCore 0:
  23.9 61.8 all-gather.4
